TPU v7x, 32 devices: a whole 2x2x4 slice. The times are simulated.
32 devices in a mesh: seg: 2 (over x), ch: 16 (over z, y, core).
Axes of the slice: x: 2, y: 2, z: 4, core: 2. Of those that a mesh axis runs over, the one named last changes fastest.
Arguments:
- recording: bfloat16 [1024, 4096], P('ch', 'seg'), parts along dimension 1, may hold values from -300 to 300
- live_mask: int32 [4096], P('seg'), parts along dimension 0, may hold values 0 or 1
- window_starts: int32 [64], P('seg'), parts along dimension 0, may hold values from 0 to 512, as said below
- source_order: int32 [4], P('seg'), parts along dimension 0, may hold values from 0 to 15
Outputs:
- correlations: bfloat16 [2, 128, 4096, 128], P(None, None, ('seg', 'ch')), parts along dimension 2
There are 2 independent parts, one for each index of `seg`. A program takes and returns all parts, laid end to end along the dimension named above; each array names one. Nothing has to cross between parts.
Inputs may be any that keep to these rules, and one draw needn't show every extreme that they name: `window_starts`: the first start is 0 and the last is 512; the others are in no order and may repeat. `source_order`: block b is the channels b * 128 to (b + 1) * 128 - 1; blocks may repeat.
All inputs are finite; a program needn't handle non-finite values.
Results may differ from a plain program's by a relative error of at most 0.0059.
Values may be sent and summed in bfloat16 or wider, within the bound.
No kernel may reach another device: no remote copies, remote signals or barrier semaphores. Data moves between devices by JAX's collectives and lax.ppermute only.
A program may use at most 128 MiB of HBM per device.

v0:
```python
import functools
import math

import jax
import jax.numpy as jnp
from jax import lax
from jax.experimental import pallas as pl
from jax.experimental.pallas import tpu as pltpu
from jax.sharding import PartitionSpec as P

CH_DEV = 128
WIN = 512
NF = 128
F0 = 4
LAGS = 128
HALF = 64
BAND = 64

STABILIZER_FLOOR = 1e-06
TILE = 128
SPAN = TILE + 2 * HALF
SRC_STEP = 32
BIN_STEP = 32
PITCH = NF + 1


def forward_rows():
    phases = (F0 + jnp.arange(NF))[:, None] * jnp.arange(WIN)[None, :] % WIN
    angles = phases.astype(jnp.float32) * (2.0 * math.pi / WIN)
    return jnp.concatenate([jnp.cos(angles), -jnp.sin(angles)], axis=0).astype(jnp.bfloat16)


def inverse_rows():
    phases = (jnp.arange(LAGS)[:, None] - LAGS // 2) * (F0 + jnp.arange(NF))[None, :] % WIN
    angles = phases.astype(jnp.float32) * (2.0 * math.pi / WIN)
    return jnp.concatenate([jnp.cos(angles), -jnp.sin(angles)], axis=1).astype(jnp.bfloat16)


def time_band():
    ahead = jnp.arange(SPAN)[None, :] - jnp.arange(TILE)[:, None]
    return ((ahead >= 0) & (ahead <= 2 * HALF)).astype(jnp.bfloat16)


def bin_band():
    apart = jnp.abs(jnp.arange(NF)[:, None] - jnp.arange(NF)[None, :])
    band = (apart <= BAND).astype(jnp.bfloat16)
    return jnp.concatenate([band, band], axis=1)


def inverse_counts(length, radius):
    at = jnp.arange(length)
    counts = jnp.minimum(at + radius + 1, length) - jnp.maximum(at - radius, 0)
    return jnp.broadcast_to((1.0 / counts.astype(jnp.float32))[:, None], (length, CH_DEV))


def pack_kernel(order_ref, x_ref, out_ref):
    blocks = out_ref.shape[0]
    numbers = order_ref.shape[0]
    for block in range(blocks):
        out_ref[block, :, :CH_DEV] = x_ref[:, block * CH_DEV : (block + 1) * CH_DEV]
        first = pl.multiple_of(order_ref[block % numbers] * CH_DEV, CH_DEV)
        out_ref[block, :, CH_DEV:] = x_ref[:, pl.ds(first, CH_DEV)]


def pack(order, recording):
    rows, channels = recording.shape
    blocks = channels // CH_DEV
    return pl.pallas_call(
        pack_kernel,
        out_shape=jax.ShapeDtypeStruct((blocks, rows, 2 * CH_DEV), recording.dtype),
        in_specs=[pl.BlockSpec(memory_space=pltpu.SMEM), pl.BlockSpec(memory_space=pltpu.VMEM)],
        out_specs=pl.BlockSpec(memory_space=pltpu.VMEM),
        name="pack",
    )(order, recording)


def whiten_kernel(
    starts_ref, block_ref, x_ref, first_ref, mask_ref, forward_ref, band_ref, bins_ref, tcount_ref, fcount_ref,
    out_ref, xf, means, cen, mag, nrm, spec,
):
    length = x_ref.shape[0]
    windows = starts_ref.shape[0]
    pairs = windows // 2
    pitch = 2 * windows + 1
    xf[...] = x_ref[...].astype(jnp.float32)
    at = lax.broadcasted_iota(jnp.int32, (windows, length), 1) - first_ref[...]
    inside = ((at >= 0) & (at < WIN)).astype(jnp.bfloat16)
    means[...] = jnp.dot(inside, x_ref[...], preferred_element_type=jnp.float32) * (1.0 / WIN)
    first = pl.multiple_of(block_ref[0] * CH_DEV, CH_DEV)
    mask = mask_ref[:, pl.ds(first, CH_DEV)].astype(jnp.float32)
    mask = jnp.concatenate([mask, mask], axis=1)
    edge = jnp.zeros((HALF, 2 * CH_DEV), jnp.bfloat16)
    mag[:HALF, :] = edge
    mag[HALF + WIN :, :] = edge
    interior = 1.0 / (2 * HALF + 1)

    def transform(pair):
        spectra = jnp.dot(forward_ref[...], nrm[...], preferred_element_type=jnp.float32)
        re, im = spectra[:NF, :], spectra[NF:, :]
        power = re * re + im * im
        amplitude = power * lax.rsqrt(jnp.maximum(power, 1e-37))
        high = amplitude.astype(jnp.bfloat16)
        low = (amplitude - high.astype(jnp.float32)).astype(jnp.bfloat16)
        sums = jnp.dot(
            bins_ref[...], jnp.concatenate([high, low], axis=0), preferred_element_type=jnp.float32
        )
        count = fcount_ref[...]
        smooth = sums * jnp.concatenate([count, count], axis=1)
        scale = mask / (smooth + STABILIZER_FLOOR)
        for part, values in enumerate((re * scale, im * scale)):
            for side in range(2):
                row = part * windows + 2 * pair + side
                spec[pl.ds(row, NF, stride=pitch), :] = values[:, side * CH_DEV : (side + 1) * CH_DEV]

    def normalize(pair):
        for side in range(2):
            lanes = slice(side * CH_DEV, (side + 1) * CH_DEV)
            window = 2 * pair + side
            centred = xf[pl.ds(starts_ref[window], WIN), :] - means[pl.ds(window, 1), :]
            cen[:, lanes] = centred
            mag[HALF : HALF + WIN, lanes] = jnp.abs(centred.astype(jnp.bfloat16))
        for tile in range(WIN // TILE):
            rows = slice(tile * TILE, (tile + 1) * TILE)
            sums = jnp.dot(
                band_ref[...], mag[tile * TILE : tile * TILE + SPAN, :], preferred_element_type=jnp.float32
            )
            if HALF <= tile * TILE and (tile + 1) * TILE <= WIN - HALF:
                running = sums * interior
            else:
                count = tcount_ref[rows, :]
                running = sums * jnp.concatenate([count, count], axis=1)
            nrm[rows, :] = (cen[rows, :] / (running + STABILIZER_FLOOR)).astype(jnp.bfloat16)

    def step(number, carry):
        transform(jnp.maximum(number - 1, 0))
        normalize(jnp.minimum(number, pairs - 1))
        return carry

    lax.fori_loop(0, pairs + 1, step, 0)

    def emit(f, carry):
        out_ref[f] = spec[pl.ds(f * pitch, 2 * windows), :].astype(jnp.bfloat16)
        return carry

    lax.fori_loop(0, NF, emit, 0, unroll=8)


def whiten(samples, column, starts, block, live_mask, tables):
    length = samples.shape[0]
    windows = starts.shape[0]
    channels = live_mask.shape[0]
    smem = pl.BlockSpec(memory_space=pltpu.SMEM)
    whole = lambda a: pl.BlockSpec(a.shape, lambda i: (0,) * a.ndim)
    return pl.pallas_call(
        whiten_kernel,
        grid=(1,),
        out_shape=jax.ShapeDtypeStruct((NF, 2 * windows, CH_DEV), jnp.bfloat16),
        in_specs=[
            smem,
            smem,
            pl.BlockSpec((length, CH_DEV), lambda i: (0, column)),
            pl.BlockSpec((windows, 1), lambda i: (0, 0)),
            pl.BlockSpec((1, channels), lambda i: (0, 0)),
        ]
        + [whole(t) for t in tables],
        out_specs=pl.BlockSpec((NF, 2 * windows, CH_DEV), lambda i: (0, 0, 0)),
        scratch_shapes=[
            pltpu.VMEM((length, CH_DEV), jnp.float32),
            pltpu.VMEM((windows, CH_DEV), jnp.float32),
            pltpu.VMEM((WIN, 2 * CH_DEV), jnp.float32),
            pltpu.VMEM((WIN + 2 * HALF, 2 * CH_DEV), jnp.bfloat16),
            pltpu.VMEM((WIN, 2 * CH_DEV), jnp.bfloat16),
            pltpu.VMEM((NF * (2 * windows + 1), CH_DEV), jnp.float32),
        ],
        cost_estimate=pl.CostEstimate(flops=6_000_000_000, bytes_accessed=3_000_000, transcendentals=0),
        name="whiten",
        compiler_params=pltpu.CompilerParams(vmem_limit_bytes=14 * 1024 * 1024),
    )(starts, block, samples, starts.reshape(windows, 1), live_mask.reshape(1, channels), *tables)


def correlate_kernel(parity_ref, here_ref, there_ref, own_ref, inverse_ref, out_ref, cross_re, cross_im, lag):
    bins, rows = own_ref.shape[0], own_ref.shape[1]
    half = rows // 2
    scale = math.sqrt(half / NF) / half
    step = pl.program_id(0)
    crossing = NF // bins

    @pl.when(step < crossing)
    def _():
        for f in range(bins):
            source = jnp.concatenate([here_ref[f], there_ref[f]], axis=1)
            own = own_ref[f]
            swapped = jnp.concatenate([own[half:], -own[:half]], axis=0)
            product = lax.dot_general(
                source,
                jnp.concatenate([own, swapped], axis=1),
                (((0,), (0,)), ((), ())),
                preferred_element_type=jnp.float32,
            )
            at = pl.ds(step * bins + f, 2 * CH_DEV, stride=PITCH)
            cross_re[at, :] = product[:, :CH_DEV]
            cross_im[at, :] = product[:, CH_DEV:]

    @pl.when(step >= crossing)
    def _():
        for s in range(SRC_STEP):
            out_ref[0, s] = lag[s].T
        chunk = jnp.minimum(step - crossing, 2 * CH_DEV // SRC_STEP - 1)
        base = chunk * SRC_STEP * PITCH
        for s in range(0, SRC_STEP, 2):
            columns = []
            for one in (s, s + 1):
                at = pl.ds(base + one * PITCH, NF)
                columns.append(
                    jnp.concatenate(
                        [cross_re[at, :].astype(jnp.bfloat16), cross_im[at, :].astype(jnp.bfloat16)], axis=0
                    )
                )
            lagged = jnp.dot(
                inverse_ref[...], jnp.concatenate(columns, axis=1), preferred_element_type=jnp.float32
            )
            lagged = (lagged * scale).astype(jnp.bfloat16)
            for side in range(2):
                lag[s + side] = lagged[:, side * CH_DEV : (side + 1) * CH_DEV]


def correlate(parity, here, there, own, inverse):
    crossing = NF // BIN_STEP
    chunks = CH_DEV // SRC_STEP
    spectrum = pl.BlockSpec((BIN_STEP,) + here.shape[1:], lambda i, p: (jnp.minimum(i, crossing - 1), 0, 0))

    def placed(i, p):
        chunk = jnp.clip(i - crossing - 1, 0, 2 * chunks - 1)
        return (chunk // chunks + p[0]) % 2, chunk % chunks, 0, 0

    return pl.pallas_call(
        correlate_kernel,
        grid_spec=pltpu.PrefetchScalarGridSpec(
            num_scalar_prefetch=1,
            grid=(crossing + 2 * chunks + 1,),
            in_specs=[spectrum, spectrum, spectrum, pl.BlockSpec(inverse.shape, lambda i, p: (0, 0))],
            out_specs=pl.BlockSpec((1, SRC_STEP, CH_DEV, LAGS), placed),
            scratch_shapes=[pltpu.VMEM((2 * CH_DEV * PITCH, CH_DEV), jnp.float32)] * 2
            + [pltpu.VMEM((SRC_STEP, LAGS, CH_DEV), jnp.bfloat16)],
        ),
        out_shape=jax.ShapeDtypeStruct((2, CH_DEV, CH_DEV, LAGS), jnp.bfloat16),
        name="correlate",
        compiler_params=pltpu.CompilerParams(vmem_limit_bytes=48 * 1024 * 1024),
    )(parity, here, there, own, inverse)


def local(recording, live_mask, window_starts, source_order):
    position = lax.axis_index("ch").astype(jnp.int32)
    parity = position % 2
    sent = pack(source_order, recording)
    arrived = lax.all_to_all(sent, "ch", split_axis=0, concat_axis=0, tiled=True)
    samples = arrived.reshape(-1, 2 * CH_DEV)
    tables = (
        forward_rows(),
        time_band(),
        bin_band(),
        inverse_counts(WIN, HALF),
        inverse_counts(NF, BAND),
    )
    own_source = lax.dynamic_slice_in_dim(source_order, parity, 1, 0)
    here = whiten(samples, 1, window_starts, own_source, live_mask, tables)
    devices = lax.axis_size("ch")
    there = lax.ppermute(here, "ch", [(i, i ^ 1) for i in range(devices)])
    own = whiten(samples, 0, window_starts, position[None], live_mask, tables)
    return correlate(parity[None], here, there, own, inverse_rows())


def solution(mesh):
    in_specs = (P("ch", "seg"), P("seg"), P("seg"), P("seg"))
    out_specs = P(None, None, ("seg", "ch"), None)
    return jax.shard_map(local, mesh=mesh, in_specs=in_specs, out_specs=out_specs, check_vma=False)
```

profile of v0, /device:TPU:0, one launch (start us, length us, event | category | flops | bytes accessed | tf_op | source)
XLA Modules:
  0.0 63.3 jit_solution(8518179878688511653)
XLA Ops:
  0.0 0.0 copy-start.1
  0.0 0.0 copy-start.2
  0.0 1.9 %pack.1 = bf16[16,64,256]{2,1,0:T(8,128)(2,1)} custom-call(s32[2]{0:T(128)} %order_ref.1, bf16[64,2048]{1,0:T(8,128)(2,1)} %x_ref.1), custom_call_target="tpu_custom_call" | custom-call | tf_op jit(solution)/shard_map/pack/pallas_call | solution.py:68
  1.9 7.4 %all-to-all-start = ((bf16[16,64,256]{2,1,0:T(8,128)(2,1)}), bf16[16,64,256]{2,1,0:T(8,128)(2,1)S(1)}, u32[]{:S(2)}, u32[]{:S(2)}) async-start(bf16[16,64,256]{2,1,0:T(8,128)(2,1)} %pack.1), calls=%async_computation | async-start | bytes 1048576 | tf_op jit(solution)/shard_map/all_to_all | solution.py:256
  9.3 1.3 %dynamic_slice.3.block_ref = s32[1]{0:T(128)} dynamic-slice(s32[2]{0:T(128)} %order_ref.1, s32[]{:T(128)S(6)} %select_n.27), dynamic_slice_sizes={1} | dynamic-slice | bytes 12 | tf_op jit(solution)/shard_map/dynamic_slice | solution.py:265
  10.6 0.7 %copy.5.first_ref = s32[32,1]{1,0:T(8,128)S(1)} copy(s32[32,1]{0,1:T(1,128)} %bitcast.7) | data formatting | bytes 256 | tf_op jit(solution)/shard_map/reshape | solution.py:178
  11.4 1.2 %cosine_convert_fusion = (bf16[128,512]{1,0:T(8,128)(2,1)S(1)}, bf16[128,512]{1,0:T(8,128)(2,1)S(1)}) fusion(s32[128]{0:T(128)S(1)} %get-tuple-element.12), kind=kLoop, calls=%fused_computation.8 | loop fusion | flops 1114112 | bytes 262656 | tf_op jit(solution)/shard_map/convert.3
  12.7 10.9 %all-to-all-done = bf16[16,64,256]{2,1,0:T(8,128)(2,1)S(1)} async-done(((bf16[16,64,256]{2,1,0:T(8,128)(2,1)}), bf16[16,64,256]{2,1,0:T(8,128)(2,1)S(1)}, u32[]{:S(2)}, u32[]{:S(2)}) %all-to-all-start) | async-done | bytes 524320 | tf_op jit(solution)/shard_map/all_to_all | solution.py:256
  23.6 0.1 broadcast_in_dim.14.fcount_ref
  23.6 0.1 broadcast_in_dim.13.tcount_ref
  23.8 0.0 copy-done.1
  23.8 0.0 copy-done.2
  23.8 12.2 %whiten.2.here_ref = bf16[128,64,128]{2,1,0:T(8,128)(2,1)S(1)} custom-call(s32[32]{0:T(128)S(1)} %copy-done.1, s32[1]{0:T(128)} %dynamic_slice.3.block_ref, bf16[1024,256]{1,0:T(8,128)(2,1)S(1)} %bitcast.5, s32[32,1]{1,0:T(8,128)S(1)} %copy.5.first_ref, s32[1,2048]{1,0:T(1,128)S(1)} %bitcast.8, bf16[256,512]{1,0:T(8,128)(2,1)S(1)} %pad_maximum_fusion.forward_ref, ...), custom_call_target="tpu_custom_call" | custom-call | flops 6000000000 | bytes 3000000 | tf_op jit(solution)/shard_map/whiten/pallas_call | solution.py:154
  36.0 0.2 collective-permute-start
  36.2 0.3 cosine_convert_fusion.1
  36.6 11.6 %whiten.3.own_ref = bf16[128,64,128]{2,1,0:T(8,128)(2,1)S(1)} custom-call(s32[32]{0:T(128)S(1)} %copy-done.1, s32[1]{0:T(128)} %bitcast.4.block_ref, bf16[1024,256]{1,0:T(8,128)(2,1)S(1)} %bitcast.6, s32[32,1]{1,0:T(8,128)S(1)} %copy.5.first_ref, s32[1,2048]{1,0:T(1,128)S(1)} %bitcast.9, bf16[256,512]{1,0:T(8,128)(2,1)S(1)} %pad_maximum_fusion.forward_ref, ...), custom_call_target="tpu_custom_call" | custom-call | flops 6000000000 | bytes 3000000 | tf_op jit(solution)/shard_map/whiten/pallas_call | solution.py:154
  48.2 0.0 copy-start
  48.2 1.3 %copy-done = bf16[128,64,128]{2,1,0:T(8,128)(2,1)} copy-done((bf16[128,64,128]{2,1,0:T(8,128)(2,1)}, bf16[128,64,128]{2,1,0:T(8,128)(2,1)S(1)}, u32[]{:S(2)}) %copy-start) | copy-done | bytes 2097176
  49.5 0.0 collective-permute-done.there_ref
  49.5 13.7 %correlate.1 = bf16[2,128,128,128]{3,2,1,0:T(8,128)(2,1)} custom-call(s32[1]{0:T(128)} %bitcast.parity_ref, bf16[128,64,128]{2,1,0:T(8,128)(2,1)S(1)} %whiten.2.here_ref, bf16[128,64,128]{2,1,0:T(8,128)(2,1)S(1)} %collective-permute-done.there_ref, bf16[128,64,128]{2,1,0:T(8,128)(2,1)} %copy-done, bf16[128,256]{1,0:T(8,128)(2,1)S(1)} %pad_maximum_fusion.1.inverse_ref), custom_call_target="tpu_custom_call" | custom-call | tf_op jit(solution)/shard_map/correlate/pallas_call | solution.py:236
  (7 shorter events, 0.1 us)
Async XLA Ops:
  0.0 23.8 %copy-start.1 = (s32[32]{0:T(128)S(1)}, s32[32]{0:T(128)}, u32[]{:S(2)}) copy-start(s32[32]{0:T(128)} %starts_ref.3) | copy-start | bytes 388
  0.0 23.8 %copy-start.2 = (s32[2048]{0:T(1024)S(1)}, s32[2048]{0:T(1024)}, u32[]{:S(2)}) copy-start(s32[2048]{0:T(1024)} %param.5) | copy-start | bytes 24580
  1.9 21.7 %all-to-all-start = ((bf16[16,64,256]{2,1,0:T(8,128)(2,1)}), bf16[16,64,256]{2,1,0:T(8,128)(2,1)S(1)}, u32[]{:S(2)}, u32[]{:S(2)}) async-start(bf16[16,64,256]{2,1,0:T(8,128)(2,1)} %pack.1), calls=%async_computation | async-start | bytes 1048576 | tf_op jit(solution)/shard_map/all_to_all | solution.py:256
  36.0 13.5 %collective-permute-start = (bf16[128,64,128]{2,1,0:T(8,128)(2,1)S(1)}, bf16[128,64,128]{2,1,0:T(8,128)(2,1)S(1)}, u32[]{:S(2)}, u32[]{:S(2)}) collective-permute-start(bf16[128,64,128]{2,1,0:T(8,128)(2,1)S(1)} %whiten.2.here_ref), channel_id=1, source_target_pairs={{0,1},{1,0},{2,3},{3,2},{4,5},{5,4},{6,7},{7,6},{8,9},{9,8},{10,11... | collective-permute-start | bytes 6291464 | tf_op jit(solution)/shard_map/ppermute | solution.py:268
  48.2 1.3 %copy-start = (bf16[128,64,128]{2,1,0:T(8,128)(2,1)}, bf16[128,64,128]{2,1,0:T(8,128)(2,1)S(1)}, u32[]{:S(2)}) copy-start(bf16[128,64,128]{2,1,0:T(8,128)(2,1)S(1)} %whiten.3.own_ref) | copy-start | bytes 6291460
where the time goes:
time: 63.5 us; the launch traced here: 63.3 us
  Pallas kernels  39.4 us (62%)
  waiting for transfers between devices  10.9 us (17%)
  starting transfers between devices  7.62 us (12%)
  local copies, waits for them, and re-layouts  3.55 us (6%)
  other arithmetic  1.7 us (3%)
    pallas_call x2, Pallas kernels, whiten(): pl.pallas_call(whiten_kernel, grid=(1,), out_shape=jax.ShapeDtypeStruct((...  23.8 us
    pallas_call x1, Pallas kernels, correlate(): pl.pallas_call(correlate_kernel, grid_spec=pltpu.PrefetchScalarGridSpec(n...  13.7 us
    all_to_all x1, waiting for transfers between devices, local(): lax.all_to_all(sent, 'ch', split_axis=0, concat_axis=0, tiled=True)  10.9 us
    all_to_all x1, starting transfers between devices, local(): lax.all_to_all(sent, 'ch', split_axis=0, concat_axis=0, tiled=True)  7.41 us
    pallas_call x1, Pallas kernels, pack(): pl.pallas_call(pack_kernel, out_shape=jax.ShapeDtypeStruct((blocks, rows,...  1.87 us
    another operation x2, other arithmetic  1.59 us
    unnamed x6, local copies, waits for them, and re-layouts  1.34 us
  transfers between devices with their start and end apart: 2, of which 1 were waited for; matrix products, arithmetic and copies ran while one was open for 6% of the time, Pallas kernels for 18%

commit v1 on v0

--- a/solution.py
+++ b/solution.py
@@ -76,7 +76,7 @@
 
 def whiten_kernel(
     starts_ref, block_ref, x_ref, first_ref, mask_ref, forward_ref, band_ref, bins_ref, tcount_ref, fcount_ref,
-    out_ref, xf, means, cen, mag, nrm, spec,
+    out_ref, xf, means, cen, mag, nrm, total, spc, spec,
 ):
     length = x_ref.shape[0]
     windows = starts_ref.shape[0]
@@ -89,14 +89,51 @@
     first = pl.multiple_of(block_ref[0] * CH_DEV, CH_DEV)
     mask = mask_ref[:, pl.ds(first, CH_DEV)].astype(jnp.float32)
     mask = jnp.concatenate([mask, mask], axis=1)
-    edge = jnp.zeros((HALF, 2 * CH_DEV), jnp.bfloat16)
-    mag[:HALF, :] = edge
-    mag[HALF + WIN :, :] = edge
+    edge = jnp.zeros((HALF, CH_DEV), jnp.bfloat16)
+    for slot in range(2):
+        for side in range(2):
+            mag[slot][side][:HALF, :] = edge
+            mag[slot][side][HALF + WIN :, :] = edge
     interior = 1.0 / (2 * HALF + 1)
 
-    def transform(pair):
-        spectra = jnp.dot(forward_ref[...], nrm[...], preferred_element_type=jnp.float32)
-        re, im = spectra[:NF, :], spectra[NF:, :]
+    def center(pair, slot):
+        for side in range(2):
+            window = 2 * pair + side
+            centred = xf[pl.ds(starts_ref[window], WIN), :] - means[pl.ds(window, 1), :]
+            cen[slot][side][...] = centred
+            mag[slot][side][HALF : HALF + WIN, :] = jnp.abs(centred).astype(jnp.bfloat16)
+
+    def band(slot):
+        for tile in range(WIN // TILE):
+            rows = slice(tile * TILE, tile * TILE + SPAN)
+            total[slot][tile * TILE : (tile + 1) * TILE, :] = jnp.dot(
+                band_ref[...],
+                jnp.concatenate([mag[slot][0][rows, :], mag[slot][1][rows, :]], axis=1),
+                preferred_element_type=jnp.float32,
+            )
+
+    def normalize(pair, slot):
+        for tile in range(WIN // TILE):
+            rows = slice(tile * TILE, (tile + 1) * TILE)
+            for side in range(2):
+                running = total[slot][rows, side * CH_DEV : (side + 1) * CH_DEV]
+                if HALF <= tile * TILE and (tile + 1) * TILE <= WIN - HALF:
+                    running = running * interior
+                else:
+                    running = running * tcount_ref[rows, :]
+                nrm[slot][side][rows, :] = (cen[slot][side][rows, :] / (running + STABILIZER_FLOOR)).astype(
+                    jnp.bfloat16
+                )
+
+    def transform(slot):
+        spc[slot][...] = jnp.dot(
+            forward_ref[...],
+            jnp.concatenate([nrm[slot][0][...], nrm[slot][1][...]], axis=1),
+            preferred_element_type=jnp.float32,
+        )
+
+    def spectral(pair, slot):
+        re, im = spc[slot][:NF, :], spc[slot][NF:, :]
         power = re * re + im * im
         amplitude = power * lax.rsqrt(jnp.maximum(power, 1e-37))
         high = amplitude.astype(jnp.bfloat16)
@@ -107,36 +144,23 @@
         count = fcount_ref[...]
         smooth = sums * jnp.concatenate([count, count], axis=1)
         scale = mask / (smooth + STABILIZER_FLOOR)
-        for part, values in enumerate((re * scale, im * scale)):
+        for part in range(2):
+            values = spc[slot][part * NF : (part + 1) * NF, :] * scale
             for side in range(2):
                 row = part * windows + 2 * pair + side
                 spec[pl.ds(row, NF, stride=pitch), :] = values[:, side * CH_DEV : (side + 1) * CH_DEV]
 
-    def normalize(pair):
-        for side in range(2):
-            lanes = slice(side * CH_DEV, (side + 1) * CH_DEV)
-            window = 2 * pair + side
-            centred = xf[pl.ds(starts_ref[window], WIN), :] - means[pl.ds(window, 1), :]
-            cen[:, lanes] = centred
-            mag[HALF : HALF + WIN, lanes] = jnp.abs(centred.astype(jnp.bfloat16))
-        for tile in range(WIN // TILE):
-            rows = slice(tile * TILE, (tile + 1) * TILE)
-            sums = jnp.dot(
-                band_ref[...], mag[tile * TILE : tile * TILE + SPAN, :], preferred_element_type=jnp.float32
-            )
-            if HALF <= tile * TILE and (tile + 1) * TILE <= WIN - HALF:
-                running = sums * interior
-            else:
-                count = tcount_ref[rows, :]
-                running = sums * jnp.concatenate([count, count], axis=1)
-            nrm[rows, :] = (cen[rows, :] / (running + STABILIZER_FLOOR)).astype(jnp.bfloat16)
-
-    def step(number, carry):
-        transform(jnp.maximum(number - 1, 0))
-        normalize(jnp.minimum(number, pairs - 1))
+    def step(index, carry):
+        for phase in range(6):
+            number, now, before = 6 * index + phase, phase % 2, (phase + 1) % 2
+            normalize(jnp.clip(number - 1, 0, pairs - 1), before)
+            transform(before)
+            center(jnp.minimum(number, pairs - 1), now)
+            band(now)
+            spectral(jnp.maximum(number - 2, 0), now)
         return carry
 
-    lax.fori_loop(0, pairs + 1, step, 0)
+    lax.fori_loop(0, (pairs + 2 + 6 - 1) // 6, step, 0)
 
     def emit(f, carry):
         out_ref[f] = spec[pl.ds(f * pitch, 2 * windows), :].astype(jnp.bfloat16)
@@ -167,9 +191,11 @@
         scratch_shapes=[
             pltpu.VMEM((length, CH_DEV), jnp.float32),
             pltpu.VMEM((windows, CH_DEV), jnp.float32),
-            pltpu.VMEM((WIN, 2 * CH_DEV), jnp.float32),
-            pltpu.VMEM((WIN + 2 * HALF, 2 * CH_DEV), jnp.bfloat16),
-            pltpu.VMEM((WIN, 2 * CH_DEV), jnp.bfloat16),
+            [[pltpu.VMEM((WIN, CH_DEV), jnp.float32)] * 2] * 2,
+            [[pltpu.VMEM((WIN + 2 * HALF, CH_DEV), jnp.bfloat16)] * 2] * 2,
+            [[pltpu.VMEM((WIN, CH_DEV), jnp.bfloat16)] * 2] * 2,
+            [pltpu.VMEM((WIN, 2 * CH_DEV), jnp.float32)] * 2,
+            [pltpu.VMEM((2 * NF, 2 * CH_DEV), jnp.float32)] * 2,
             pltpu.VMEM((NF * (2 * windows + 1), CH_DEV), jnp.float32),
         ],
         cost_estimate=pl.CostEstimate(flops=6_000_000_000, bytes_accessed=3_000_000, transcendentals=0),
@@ -245,7 +271,7 @@
         ),
         out_shape=jax.ShapeDtypeStruct((2, CH_DEV, CH_DEV, LAGS), jnp.bfloat16),
         name="correlate",
-        compiler_params=pltpu.CompilerParams(vmem_limit_bytes=48 * 1024 * 1024),
+        compiler_params=pltpu.CompilerParams(vmem_limit_bytes=40 * 1024 * 1024),
     )(parity, here, there, own, inverse)
 
 

time: 63.5 us -> 52.7 us (0.83)
  Pallas kernels: 39.4 us -> 29.9 us
  local copies, waits for them, and re-layouts: 3.55 us -> 2.21 us
    pallas_call x2, Pallas kernels: 23.8 us -> 15.4 us  [whiten(): pl.pallas_call(whiten_kernel, grid=(1,), out_shape=jax.ShapeDtypeStruct((...]
    unnamed x6 -> x4, local copies, waits for them, and re-layouts: 1.34 us -> 0.01 us
    pallas_call x1, Pallas kernels: 13.7 us -> 12.6 us  [correlate(): pl.pallas_call(correlate_kernel, grid_spec=pltpu.PrefetchScalarGridSpec(n...]
  transfers between devices with their start and end apart: 2 -> 2, of which waited for: 1 -> 1; matrix products, arithmetic and copies ran while one was open for 6% -> 7% of each run, Pallas kernels for 18% -> 14%
where the time goes in v1:
time: 52.7 us; the launch traced here: 52.4 us
  Pallas kernels  29.9 us (57%)
  waiting for transfers between devices  10.9 us (21%)
  starting transfers between devices  7.62 us (14%)
  local copies, waits for them, and re-layouts  2.21 us (4%)
  other arithmetic  1.7 us (3%)
    pallas_call x2, Pallas kernels, whiten(): pl.pallas_call(whiten_kernel, grid=(1,), out_shape=jax.ShapeDtypeStruct((...  15.4 us
    pallas_call x1, Pallas kernels, correlate(): pl.pallas_call(correlate_kernel, grid_spec=pltpu.PrefetchScalarGridSpec(n...  12.6 us
    all_to_all x1, waiting for transfers between devices, local(): lax.all_to_all(sent, 'ch', split_axis=0, concat_axis=0, tiled=True)  10.9 us
    all_to_all x1, starting transfers between devices, local(): lax.all_to_all(sent, 'ch', split_axis=0, concat_axis=0, tiled=True)  7.41 us
    pallas_call x1, Pallas kernels, pack(): pl.pallas_call(pack_kernel, out_shape=jax.ShapeDtypeStruct((blocks, rows,...  1.88 us
    another operation x2, other arithmetic  1.59 us
    dynamic_slice x1, local copies, waits for them, and re-layouts, local(): own_source = lax.dynamic_slice_in_dim(source_order, parity, 1, 0)  1.27 us
  transfers between devices with their start and end apart: 2, of which 1 were waited for; matrix products, arithmetic and copies ran while one was open for 7% of the time, Pallas kernels for 14%

profile of v1, /device:TPU:0, one launch (start us, length us, event | category | flops | bytes accessed | tf_op | source)
XLA Modules:
  0.0 52.4 jit_solution(2348066367797023809)
XLA Ops:
  0.0 0.0 copy-start
  0.0 0.0 copy-start.1
  0.0 1.9 %pack.1 = bf16[16,64,256]{2,1,0:T(8,128)(2,1)} custom-call(s32[2]{0:T(128)} %order_ref.1, bf16[64,2048]{1,0:T(8,128)(2,1)} %x_ref.1), custom_call_target="tpu_custom_call" | custom-call | tf_op jit(solution)/shard_map/pack/pallas_call | solution.py:68
  1.9 7.4 %all-to-all-start = ((bf16[16,64,256]{2,1,0:T(8,128)(2,1)}), bf16[16,64,256]{2,1,0:T(8,128)(2,1)S(1)}, u32[]{:S(2)}, u32[]{:S(2)}) async-start(bf16[16,64,256]{2,1,0:T(8,128)(2,1)} %pack.1), calls=%async_computation | async-start | bytes 1048576 | tf_op jit(solution)/shard_map/all_to_all | solution.py:282
  9.3 1.3 %dynamic_slice.3.block_ref = s32[1]{0:T(128)} dynamic-slice(s32[2]{0:T(128)} %order_ref.1, s32[]{:T(128)S(6)} %select_n.27), dynamic_slice_sizes={1} | dynamic-slice | bytes 12 | tf_op jit(solution)/shard_map/dynamic_slice | solution.py:291
  10.6 0.7 %copy.5.first_ref = s32[32,1]{1,0:T(8,128)S(1)} copy(s32[32,1]{0,1:T(1,128)} %bitcast.7) | data formatting | bytes 256 | tf_op jit(solution)/shard_map/reshape | solution.py:204
  11.4 1.2 %cosine_convert_fusion = (bf16[128,512]{1,0:T(8,128)(2,1)S(1)}, bf16[128,512]{1,0:T(8,128)(2,1)S(1)}) fusion(s32[128]{0:T(128)S(1)} %get-tuple-element.12), kind=kLoop, calls=%fused_computation.8 | loop fusion | flops 1114112 | bytes 262656 | tf_op jit(solution)/shard_map/convert.3
  12.7 10.9 %all-to-all-done = bf16[16,64,256]{2,1,0:T(8,128)(2,1)S(1)} async-done(((bf16[16,64,256]{2,1,0:T(8,128)(2,1)}), bf16[16,64,256]{2,1,0:T(8,128)(2,1)S(1)}, u32[]{:S(2)}, u32[]{:S(2)}) %all-to-all-start) | async-done | bytes 524320 | tf_op jit(solution)/shard_map/all_to_all | solution.py:282
  23.6 0.1 broadcast_in_dim.14.fcount_ref
  23.6 0.1 broadcast_in_dim.13.tcount_ref
  23.8 0.0 copy-done
  23.8 0.0 copy-done.1
  23.8 8.0 %whiten.2.here_ref = bf16[128,64,128]{2,1,0:T(8,128)(2,1)S(1)} custom-call(s32[32]{0:T(128)S(1)} %copy-done, s32[1]{0:T(128)} %dynamic_slice.3.block_ref, bf16[1024,256]{1,0:T(8,128)(2,1)S(1)} %bitcast.5, s32[32,1]{1,0:T(8,128)S(1)} %copy.5.first_ref, s32[1,2048]{1,0:T(1,128)S(1)} %bitcast.8, bf16[256,512]{1,0:T(8,128)(2,1)S(1)} %pad_maximum_fusion.forward_ref, ...), custom_call_target="tpu_custom_call" | custom-call | flops 6000000000 | bytes 3000000 | tf_op jit(solution)/shard_map/whiten/pallas_call | solution.py:178
  31.8 0.2 collective-permute-start
  32.0 0.3 cosine_convert_fusion.1
  32.4 7.4 %whiten.3.own_ref = bf16[128,64,128]{2,1,0:T(8,128)(2,1)S(1)} custom-call(s32[32]{0:T(128)S(1)} %copy-done, s32[1]{0:T(128)} %bitcast.4.block_ref, bf16[1024,256]{1,0:T(8,128)(2,1)S(1)} %bitcast.6, s32[32,1]{1,0:T(8,128)S(1)} %copy.5.first_ref, s32[1,2048]{1,0:T(1,128)S(1)} %bitcast.9, bf16[256,512]{1,0:T(8,128)(2,1)S(1)} %pad_maximum_fusion.forward_ref, ...), custom_call_target="tpu_custom_call" | custom-call | flops 6000000000 | bytes 3000000 | tf_op jit(solution)/shard_map/whiten/pallas_call | solution.py:178
  39.8 0.0 collective-permute-done.there_ref
  39.8 12.6 %correlate.1 = bf16[2,128,128,128]{3,2,1,0:T(8,128)(2,1)} custom-call(s32[1]{0:T(128)} %bitcast.parity_ref, bf16[128,64,128]{2,1,0:T(8,128)(2,1)S(1)} %whiten.2.here_ref, bf16[128,64,128]{2,1,0:T(8,128)(2,1)S(1)} %collective-permute-done.there_ref, bf16[128,64,128]{2,1,0:T(8,128)(2,1)S(1)} %whiten.3.own_ref, bf16[128,256]{1,0:T(8,128)(2,1)S(1)} %pad_maximum_fusion.1.inverse_ref), custom_call_target="tpu_custom_call" | custom-call | tf_op jit(solution)/shard_map/correlate/pallas_call | solution.py:262
  (7 shorter events, 0.1 us)
Async XLA Ops:
  0.0 23.8 %copy-start = (s32[32]{0:T(128)S(1)}, s32[32]{0:T(128)}, u32[]{:S(2)}) copy-start(s32[32]{0:T(128)} %starts_ref.3) | copy-start | bytes 388
  0.0 23.8 %copy-start.1 = (s32[2048]{0:T(1024)S(1)}, s32[2048]{0:T(1024)}, u32[]{:S(2)}) copy-start(s32[2048]{0:T(1024)} %param.5) | copy-start | bytes 24580
  1.9 21.7 %all-to-all-start = ((bf16[16,64,256]{2,1,0:T(8,128)(2,1)}), bf16[16,64,256]{2,1,0:T(8,128)(2,1)S(1)}, u32[]{:S(2)}, u32[]{:S(2)}) async-start(bf16[16,64,256]{2,1,0:T(8,128)(2,1)} %pack.1), calls=%async_computation | async-start | bytes 1048576 | tf_op jit(solution)/shard_map/all_to_all | solution.py:282
  31.8 8.0 %collective-permute-start = (bf16[128,64,128]{2,1,0:T(8,128)(2,1)S(1)}, bf16[128,64,128]{2,1,0:T(8,128)(2,1)S(1)}, u32[]{:S(2)}, u32[]{:S(2)}) collective-permute-start(bf16[128,64,128]{2,1,0:T(8,128)(2,1)S(1)} %whiten.2.here_ref), channel_id=1, source_target_pairs={{0,1},{1,0},{2,3},{3,2},{4,5},{5,4},{6,7},{7,6},{8,9},{9,8},{10,11... | collective-permute-start | bytes 6291464 | tf_op jit(solution)/shard_map/ppermute | solution.py:294

commit v2 on v1

--- a/solution.py
+++ b/solution.py
@@ -30,10 +30,11 @@
     return jnp.concatenate([jnp.cos(angles), -jnp.sin(angles)], axis=0).astype(jnp.bfloat16)
 
 
-def inverse_rows():
+def inverse_rows(scale):
     phases = (jnp.arange(LAGS)[:, None] - LAGS // 2) * (F0 + jnp.arange(NF))[None, :] % WIN
     angles = phases.astype(jnp.float32) * (2.0 * math.pi / WIN)
-    return jnp.concatenate([jnp.cos(angles), -jnp.sin(angles)], axis=1).astype(jnp.bfloat16)
+    rows = jnp.concatenate([jnp.cos(angles), -jnp.sin(angles)], axis=1).astype(jnp.bfloat16)
+    return rows * jnp.bfloat16(scale)
 
 
 def time_band():
@@ -75,20 +76,21 @@
 
 
 def whiten_kernel(
-    starts_ref, block_ref, x_ref, first_ref, mask_ref, forward_ref, band_ref, bins_ref, tcount_ref, fcount_ref,
-    out_ref, xf, means, cen, mag, nrm, total, spc, spec,
+    column, rounded, starts_ref, block_ref, x_ref, first_ref, mask_ref, forward_ref, band_ref, bins_ref, tcount_ref, fcount_ref,
+    out_ref, xf, means, cen, mag, nrm, total, spc, *scratch,
 ):
+    spec = scratch[0] if rounded else out_ref
     length = x_ref.shape[0]
     windows = starts_ref.shape[0]
     pairs = windows // 2
     pitch = 2 * windows + 1
-    xf[...] = x_ref[...].astype(jnp.float32)
+    first = pl.multiple_of(block_ref[0] * CH_DEV, CH_DEV)
+    mask = mask_ref[:, pl.ds(first, CH_DEV)]
+    samples = x_ref[:, column * CH_DEV : (column + 1) * CH_DEV].astype(jnp.float32) * mask
+    xf[...] = samples
     at = lax.broadcasted_iota(jnp.int32, (windows, length), 1) - first_ref[...]
     inside = ((at >= 0) & (at < WIN)).astype(jnp.bfloat16)
-    means[...] = jnp.dot(inside, x_ref[...], preferred_element_type=jnp.float32) * (1.0 / WIN)
-    first = pl.multiple_of(block_ref[0] * CH_DEV, CH_DEV)
-    mask = mask_ref[:, pl.ds(first, CH_DEV)].astype(jnp.float32)
-    mask = jnp.concatenate([mask, mask], axis=1)
+    means[...] = jnp.dot(inside, samples.astype(jnp.bfloat16), preferred_element_type=jnp.float32) * (1.0 / WIN)
     edge = jnp.zeros((HALF, CH_DEV), jnp.bfloat16)
     for slot in range(2):
         for side in range(2):
@@ -143,51 +145,44 @@
         )
         count = fcount_ref[...]
         smooth = sums * jnp.concatenate([count, count], axis=1)
-        scale = mask / (smooth + STABILIZER_FLOOR)
+        scale = 1.0 / (smooth + STABILIZER_FLOOR)
         for part in range(2):
             values = spc[slot][part * NF : (part + 1) * NF, :] * scale
             for side in range(2):
                 row = part * windows + 2 * pair + side
                 spec[pl.ds(row, NF, stride=pitch), :] = values[:, side * CH_DEV : (side + 1) * CH_DEV]
 
-    def step(index, carry):
-        for phase in range(6):
-            number, now, before = 6 * index + phase, phase % 2, (phase + 1) % 2
-            normalize(jnp.clip(number - 1, 0, pairs - 1), before)
+    for number in range(pairs + 2):
+        now, before = number % 2, (number + 1) % 2
+        if 1 <= number <= pairs:
+            normalize(number - 1, before)
             transform(before)
-            center(jnp.minimum(number, pairs - 1), now)
+        if number < pairs:
+            center(number, now)
             band(now)
-            spectral(jnp.maximum(number - 2, 0), now)
-        return carry
-
-    lax.fori_loop(0, (pairs + 2 + 6 - 1) // 6, step, 0)
-
-    def emit(f, carry):
-        out_ref[f] = spec[pl.ds(f * pitch, 2 * windows), :].astype(jnp.bfloat16)
-        return carry
-
-    lax.fori_loop(0, NF, emit, 0, unroll=8)
-
-
-def whiten(samples, column, starts, block, live_mask, tables):
+        if number >= 2:
+            spectral(number - 2, now)
+
+    if rounded:
+
+        def emit(f, carry):
+            out_ref[f] = spec[pl.ds(f * pitch, 2 * windows), :].astype(jnp.bfloat16)
+            return carry
+
+        lax.fori_loop(0, NF, emit, 0, unroll=8)
+
+
+def whiten(samples, column, rounded, starts, block, mask, tables):
     length = samples.shape[0]
     windows = starts.shape[0]
-    channels = live_mask.shape[0]
     smem = pl.BlockSpec(memory_space=pltpu.SMEM)
-    whole = lambda a: pl.BlockSpec(a.shape, lambda i: (0,) * a.ndim)
+    vmem = pl.BlockSpec(memory_space=pltpu.VMEM)
+    padded = pltpu.VMEM((NF * (2 * windows + 1), CH_DEV), jnp.float32)
     return pl.pallas_call(
-        whiten_kernel,
-        grid=(1,),
-        out_shape=jax.ShapeDtypeStruct((NF, 2 * windows, CH_DEV), jnp.bfloat16),
-        in_specs=[
-            smem,
-            smem,
-            pl.BlockSpec((length, CH_DEV), lambda i: (0, column)),
-            pl.BlockSpec((windows, 1), lambda i: (0, 0)),
-            pl.BlockSpec((1, channels), lambda i: (0, 0)),
-        ]
-        + [whole(t) for t in tables],
-        out_specs=pl.BlockSpec((NF, 2 * windows, CH_DEV), lambda i: (0, 0, 0)),
+        functools.partial(whiten_kernel, column, rounded),
+        out_shape=pltpu.VMEM((NF, 2 * windows, CH_DEV), jnp.bfloat16) if rounded else padded,
+        in_specs=[smem, smem] + [vmem] * (3 + len(tables)),
+        out_specs=vmem,
         scratch_shapes=[
             pltpu.VMEM((length, CH_DEV), jnp.float32),
             pltpu.VMEM((windows, CH_DEV), jnp.float32),
@@ -196,26 +191,26 @@
             [[pltpu.VMEM((WIN, CH_DEV), jnp.bfloat16)] * 2] * 2,
             [pltpu.VMEM((WIN, 2 * CH_DEV), jnp.float32)] * 2,
             [pltpu.VMEM((2 * NF, 2 * CH_DEV), jnp.float32)] * 2,
-            pltpu.VMEM((NF * (2 * windows + 1), CH_DEV), jnp.float32),
-        ],
+        ]
+        + [padded] * rounded,
         cost_estimate=pl.CostEstimate(flops=6_000_000_000, bytes_accessed=3_000_000, transcendentals=0),
         name="whiten",
         compiler_params=pltpu.CompilerParams(vmem_limit_bytes=14 * 1024 * 1024),
-    )(starts, block, samples, starts.reshape(windows, 1), live_mask.reshape(1, channels), *tables)
+    )(starts, block, samples, starts.reshape(windows, 1), mask, *tables)
 
 
 def correlate_kernel(parity_ref, here_ref, there_ref, own_ref, inverse_ref, out_ref, cross_re, cross_im, lag):
-    bins, rows = own_ref.shape[0], own_ref.shape[1]
+    bins, rows = BIN_STEP, here_ref.shape[1]
     half = rows // 2
-    scale = math.sqrt(half / NF) / half
     step = pl.program_id(0)
     crossing = NF // bins
 
     @pl.when(step < crossing)
     def _():
         for f in range(bins):
-            source = jnp.concatenate([here_ref[f], there_ref[f]], axis=1)
-            own = own_ref[f]
+            at = step * bins + f
+            source = jnp.concatenate([here_ref[at], there_ref[at]], axis=1)
+            own = own_ref[pl.ds(at * (rows + 1), rows), :].astype(jnp.bfloat16)
             swapped = jnp.concatenate([own[half:], -own[:half]], axis=0)
             product = lax.dot_general(
                 source,
@@ -245,7 +240,7 @@
             lagged = jnp.dot(
                 inverse_ref[...], jnp.concatenate(columns, axis=1), preferred_element_type=jnp.float32
             )
-            lagged = (lagged * scale).astype(jnp.bfloat16)
+            lagged = lagged.astype(jnp.bfloat16)
             for side in range(2):
                 lag[s + side] = lagged[:, side * CH_DEV : (side + 1) * CH_DEV]
 
@@ -253,7 +248,7 @@
 def correlate(parity, here, there, own, inverse):
     crossing = NF // BIN_STEP
     chunks = CH_DEV // SRC_STEP
-    spectrum = pl.BlockSpec((BIN_STEP,) + here.shape[1:], lambda i, p: (jnp.minimum(i, crossing - 1), 0, 0))
+    spectrum = pl.BlockSpec(memory_space=pltpu.VMEM)
 
     def placed(i, p):
         chunk = jnp.clip(i - crossing - 1, 0, 2 * chunks - 1)
@@ -276,24 +271,30 @@
 
 
 def local(recording, live_mask, window_starts, source_order):
+    windows = window_starts.shape[0]
     position = lax.axis_index("ch").astype(jnp.int32)
     parity = position % 2
     sent = pack(source_order, recording)
     arrived = lax.all_to_all(sent, "ch", split_axis=0, concat_axis=0, tiled=True)
     samples = arrived.reshape(-1, 2 * CH_DEV)
-    tables = (
-        forward_rows(),
-        time_band(),
-        bin_band(),
-        inverse_counts(WIN, HALF),
-        inverse_counts(NF, BAND),
+    starts, mask, inverse, *tables = lax.optimization_barrier(
+        (
+            jnp.clip(window_starts, 0, samples.shape[0] - WIN),
+            live_mask.astype(jnp.float32)[None, :],
+            inverse_rows(math.sqrt(windows / NF) / windows),
+            forward_rows(),
+            time_band(),
+            bin_band(),
+            inverse_counts(WIN, HALF),
+            inverse_counts(NF, BAND),
+        )
     )
     own_source = lax.dynamic_slice_in_dim(source_order, parity, 1, 0)
-    here = whiten(samples, 1, window_starts, own_source, live_mask, tables)
+    here = whiten(samples, 1, True, starts, own_source, mask, tables)
     devices = lax.axis_size("ch")
     there = lax.ppermute(here, "ch", [(i, i ^ 1) for i in range(devices)])
-    own = whiten(samples, 0, window_starts, position[None], live_mask, tables)
-    return correlate(parity[None], here, there, own, inverse_rows())
+    own = whiten(samples, 0, False, starts, position[None], mask, tables)
+    return correlate(parity[None], here, there, own, inverse)
 
 
 def solution(mesh):

time: 52.7 us -> 49.6 us (0.941)
  Pallas kernels: 29.9 us -> 27.4 us
  waiting for transfers between devices: 10.9 us -> 9.52 us
  other arithmetic: 1.7 us -> 3.07 us
  local copies, waits for them, and re-layouts: 2.21 us -> 1.6 us
    pallas_call x2, Pallas kernels: 15.4 us -> 13 us  [whiten(): pl.pallas_call(functools.partial(whiten_kernel, column, rounded), out_sha...]
    all_to_all x1, waiting for transfers between devices: 10.9 us -> 9.51 us  [local(): lax.all_to_all(sent, 'ch', split_axis=0, concat_axis=0, tiled=True)]
    convert_element_type x0 -> x1, other arithmetic: none -> 0.7 us  [local(): live_mask.astype(jnp.float32)[None, :]]
    min x0 -> x1, other arithmetic: none -> 0.66 us  [local(): jnp.clip(window_starts, 0, samples.shape[0] - WIN)]
    reshape x1, local copies, waits for them, and re-layouts: 0.74 us -> 0.09 us  [whiten(): starts.reshape(windows, 1)]
  transfers between devices with their start and end apart: 2 -> 2, of which waited for: 1 -> 1; matrix products, arithmetic and copies ran while one was open for 7% -> 9% of each run, Pallas kernels for 14% -> 12%
where the time goes in v2:
time: 49.6 us; the launch traced here: 49.3 us
  Pallas kernels  27.4 us (55%)
  waiting for transfers between devices  9.52 us (19%)
  starting transfers between devices  7.62 us (15%)
  other arithmetic  3.07 us (6%)
  local copies, waits for them, and re-layouts  1.6 us (3%)
    pallas_call x2, Pallas kernels, whiten(): pl.pallas_call(functools.partial(whiten_kernel, column, rounded), out_sha...  13 us
    pallas_call x1, Pallas kernels, correlate(): pl.pallas_call(correlate_kernel, grid_spec=pltpu.PrefetchScalarGridSpec(n...  12.5 us
    all_to_all x1, waiting for transfers between devices, local(): lax.all_to_all(sent, 'ch', split_axis=0, concat_axis=0, tiled=True)  9.51 us
    all_to_all x1, starting transfers between devices, local(): lax.all_to_all(sent, 'ch', split_axis=0, concat_axis=0, tiled=True)  7.41 us
    pallas_call x1, Pallas kernels, pack(): pl.pallas_call(pack_kernel, out_shape=jax.ShapeDtypeStruct((blocks, rows,...  1.85 us
    another operation x2, other arithmetic  1.59 us
    dynamic_slice x1, local copies, waits for them, and re-layouts, local(): own_source = lax.dynamic_slice_in_dim(source_order, parity, 1, 0)  1.31 us
  transfers between devices with their start and end apart: 2, of which 1 were waited for; matrix products, arithmetic and copies ran while one was open for 9% of the time, Pallas kernels for 12%

profile of v2, /device:TPU:0, one launch (start us, length us, event | category | flops | bytes accessed | tf_op | source)
XLA Modules:
  0.0 49.3 jit_solution(457373335156651251)
XLA Ops:
  0.0 1.8 %pack.1 = bf16[16,64,256]{2,1,0:T(8,128)(2,1)} custom-call(s32[2]{0:T(128)} %order_ref.1, bf16[64,2048]{1,0:T(8,128)(2,1)} %x_ref.1), custom_call_target="tpu_custom_call" | custom-call | tf_op jit(solution)/shard_map/pack/pallas_call | solution.py:69
  1.8 7.4 %all-to-all-start = ((bf16[16,64,256]{2,1,0:T(8,128)(2,1)}), bf16[16,64,256]{2,1,0:T(8,128)(2,1)S(1)}, u32[]{:S(2)}, u32[]{:S(2)}) async-start(bf16[16,64,256]{2,1,0:T(8,128)(2,1)} %pack.1), calls=%async_computation | async-start | bytes 1048576 | tf_op jit(solution)/shard_map/all_to_all | solution.py:278
  9.4 1.3 %dynamic_slice.3.block_ref = s32[1]{0:T(128)} dynamic-slice(s32[2]{0:T(128)} %order_ref.1, s32[]{:T(128)S(6)} %select_n.29), dynamic_slice_sizes={1} | dynamic-slice | bytes 12 | tf_op jit(solution)/shard_map/dynamic_slice | solution.py:292
  10.7 0.7 %convert_element_type.33 = f32[2048]{0:T(1024)S(1)} convert(s32[2048]{0:T(1024)} %param.5) | non-fusion elementwise | flops 2048 | bytes 16384 | tf_op jit(solution)/shard_map/convert_element_type | solution.py:283
  11.4 0.3 cosine_convert_fusion.1
  11.8 1.2 %cosine_convert_fusion = (bf16[128,512]{1,0:T(8,128)(2,1)S(1)}, bf16[128,512]{1,0:T(8,128)(2,1)S(1)}) fusion(s32[128]{0:T(128)S(1)} %get-tuple-element.25), kind=kLoop, calls=%fused_computation.8 | loop fusion | flops 1114112 | bytes 262656 | tf_op jit(solution)/shard_map/convert.1
  13.1 0.7 %broadcast_clamp_fusion.starts_ref = s32[32]{0:T(128)S(1)} fusion(s32[32]{0:T(128)} %param.6), kind=kLoop, calls=%fused_computation.40 | loop fusion | flops 32 | bytes 256 | tf_op jit(solution)/shard_map/jit(clip)/min | solution.py:282
  13.7 0.1 broadcast_in_dim.13.fcount_ref
  13.8 0.1 broadcast_in_dim.12.tcount_ref
  13.9 0.1 copy.5.first_ref
  14.0 9.5 %all-to-all-done = bf16[16,64,256]{2,1,0:T(8,128)(2,1)S(1)} async-done(((bf16[16,64,256]{2,1,0:T(8,128)(2,1)}), bf16[16,64,256]{2,1,0:T(8,128)(2,1)S(1)}, u32[]{:S(2)}, u32[]{:S(2)}) %all-to-all-start) | async-done | bytes 524320 | tf_op jit(solution)/shard_map/all_to_all | solution.py:278
  23.5 7.0 %whiten.2.here_ref = bf16[128,64,128]{2,1,0:T(8,128)(2,1)S(1)} custom-call(s32[32]{0:T(128)S(1)} %broadcast_clamp_fusion.starts_ref, s32[1]{0:T(128)} %dynamic_slice.3.block_ref, bf16[1024,256]{1,0:T(8,128)(2,1)S(1)} %bitcast.5, s32[32,1]{1,0:T(8,128)S(1)} %copy.5.first_ref, f32[1,2048]{1,0:T(1,128)S(1)} %bitcast.7, ...), custom_call_target="tpu_custom_call" | custom-call | flops 6000000000 | bytes 3000000 | tf_op jit(solution)/shard_map/whiten/pallas_call | solution.py:181
  30.6 0.2 collective-permute-start
  30.8 6.0 %whiten.3.own_ref = f32[8320,128]{1,0:T(8,128)S(1)} custom-call(s32[32]{0:T(128)S(1)} %broadcast_clamp_fusion.starts_ref, s32[1]{0:T(128)} %bitcast.4.block_ref, bf16[1024,256]{1,0:T(8,128)(2,1)S(1)} %bitcast.6, s32[32,1]{1,0:T(8,128)S(1)} %copy.5.first_ref, f32[1,2048]{1,0:T(1,128)S(1)} %bitcast.8, bf16[256,512]{1,0:T(8,128)(2,1)S(1)} %pad_maximum_fusion.forward_ref, ...), custom_call_target="tpu_custom_call" | custom-call | flops 6000000000 | bytes 3000000 | tf_op jit(solution)/shard_map/whiten/pallas_call | solution.py:181
  36.8 0.0 collective-permute-done.there_ref
  36.8 12.5 %correlate.1 = bf16[2,128,128,128]{3,2,1,0:T(8,128)(2,1)} custom-call(s32[1]{0:T(128)} %bitcast.parity_ref, bf16[128,64,128]{2,1,0:T(8,128)(2,1)S(1)} %whiten.2.here_ref, bf16[128,64,128]{2,1,0:T(8,128)(2,1)S(1)} %collective-permute-done.there_ref, f32[8320,128]{1,0:T(8,128)S(1)} %whiten.3.own_ref, bf16[128,256]{1,0:T(8,128)(2,1)S(1)} %maximum_multiply_fusion.inverse_ref), custom_call_target="tpu_custom_call" | custom-call | tf_op jit(solution)/shard_map/correlate/pallas_call | solution.py:257
  (7 shorter events, 0.1 us)
Async XLA Ops:
  1.8 21.7 %all-to-all-start = ((bf16[16,64,256]{2,1,0:T(8,128)(2,1)}), bf16[16,64,256]{2,1,0:T(8,128)(2,1)S(1)}, u32[]{:S(2)}, u32[]{:S(2)}) async-start(bf16[16,64,256]{2,1,0:T(8,128)(2,1)} %pack.1), calls=%async_computation | async-start | bytes 1048576 | tf_op jit(solution)/shard_map/all_to_all | solution.py:278
  30.6 6.3 %collective-permute-start = (bf16[128,64,128]{2,1,0:T(8,128)(2,1)S(1)}, bf16[128,64,128]{2,1,0:T(8,128)(2,1)S(1)}, u32[]{:S(2)}, u32[]{:S(2)}) collective-permute-start(bf16[128,64,128]{2,1,0:T(8,128)(2,1)S(1)} %whiten.2.here_ref), channel_id=1, source_target_pairs={{0,1},{1,0},{2,3},{3,2},{4,5},{5,4},{6,7},{7,6},{8,9},{9,8},{10,11... | collective-permute-start | bytes 6291464 | tf_op jit(solution)/shard_map/ppermute | solution.py:295

commit v3 on v2

--- a/solution.py
+++ b/solution.py
@@ -19,8 +19,9 @@
 STABILIZER_FLOOR = 1e-06
 TILE = 128
 SPAN = TILE + 2 * HALF
-SRC_STEP = 32
-BIN_STEP = 32
+SRC_STEP = 128
+PIECE = 16
+BIN_STEP = 64
 PITCH = NF + 1
 
 
@@ -199,16 +200,15 @@
     )(starts, block, samples, starts.reshape(windows, 1), mask, *tables)
 
 
-def correlate_kernel(parity_ref, here_ref, there_ref, own_ref, inverse_ref, out_ref, cross_re, cross_im, lag):
-    bins, rows = BIN_STEP, here_ref.shape[1]
+def correlate_kernel(
+    parity_ref, here_ref, there_ref, own_ref, inverse_ref, out_ref, cross_re, cross_im, lags, sent
+):
+    rows = here_ref.shape[1]
     half = rows // 2
-    step = pl.program_id(0)
-    crossing = NF // bins
-
-    @pl.when(step < crossing)
-    def _():
-        for f in range(bins):
-            at = step * bins + f
+
+    def cross(step, carry):
+        for f in range(BIN_STEP):
+            at = step * BIN_STEP + f
             source = jnp.concatenate([here_ref[at], there_ref[at]], axis=1)
             own = own_ref[pl.ds(at * (rows + 1), rows), :].astype(jnp.bfloat16)
             swapped = jnp.concatenate([own[half:], -own[:half]], axis=0)
@@ -218,20 +218,25 @@
                 (((0,), (0,)), ((), ())),
                 preferred_element_type=jnp.float32,
             )
-            at = pl.ds(step * bins + f, 2 * CH_DEV, stride=PITCH)
-            cross_re[at, :] = product[:, :CH_DEV]
-            cross_im[at, :] = product[:, CH_DEV:]
-
-    @pl.when(step >= crossing)
-    def _():
-        for s in range(SRC_STEP):
-            out_ref[0, s] = lag[s].T
-        chunk = jnp.minimum(step - crossing, 2 * CH_DEV // SRC_STEP - 1)
-        base = chunk * SRC_STEP * PITCH
+            to = pl.ds(at, 2 * CH_DEV, stride=PITCH)
+            cross_re[to, :] = product[:, :CH_DEV]
+            cross_im[to, :] = product[:, CH_DEV:]
+        return carry
+
+    lax.fori_loop(0, NF // BIN_STEP, cross, 0)
+
+    def copy(first):
+        block, source = (first // CH_DEV + parity_ref[0]) % 2, first % CH_DEV
+        return pltpu.make_async_copy(
+            lags.at[pl.ds(first, PIECE)], out_ref.at[block, pl.ds(source, PIECE)], sent.at[first // PIECE]
+        )
+
+    def lag(step, carry):
+        first = step * SRC_STEP
         for s in range(0, SRC_STEP, 2):
             columns = []
             for one in (s, s + 1):
-                at = pl.ds(base + one * PITCH, NF)
+                at = pl.ds((first + one) * PITCH, NF)
                 columns.append(
                     jnp.concatenate(
                         [cross_re[at, :].astype(jnp.bfloat16), cross_im[at, :].astype(jnp.bfloat16)], axis=0
@@ -239,34 +244,32 @@
                 )
             lagged = jnp.dot(
                 inverse_ref[...], jnp.concatenate(columns, axis=1), preferred_element_type=jnp.float32
-            )
-            lagged = lagged.astype(jnp.bfloat16)
+            ).astype(jnp.bfloat16)
             for side in range(2):
-                lag[s + side] = lagged[:, side * CH_DEV : (side + 1) * CH_DEV]
+                lags[first + s + side] = lagged[:, side * CH_DEV : (side + 1) * CH_DEV].T
+            if (s + 2) % PIECE == 0:
+                copy(first + s + 2 - PIECE).start()
+        return carry
+
+    lax.fori_loop(0, 2 * CH_DEV // SRC_STEP, lag, 0)
+    for number in range(2 * CH_DEV // PIECE):
+        copy(number * PIECE).wait()
 
 
 def correlate(parity, here, there, own, inverse):
-    crossing = NF // BIN_STEP
-    chunks = CH_DEV // SRC_STEP
-    spectrum = pl.BlockSpec(memory_space=pltpu.VMEM)
-
-    def placed(i, p):
-        chunk = jnp.clip(i - crossing - 1, 0, 2 * chunks - 1)
-        return (chunk // chunks + p[0]) % 2, chunk % chunks, 0, 0
-
+    vmem = pl.BlockSpec(memory_space=pltpu.VMEM)
     return pl.pallas_call(
         correlate_kernel,
-        grid_spec=pltpu.PrefetchScalarGridSpec(
-            num_scalar_prefetch=1,
-            grid=(crossing + 2 * chunks + 1,),
-            in_specs=[spectrum, spectrum, spectrum, pl.BlockSpec(inverse.shape, lambda i, p: (0, 0))],
-            out_specs=pl.BlockSpec((1, SRC_STEP, CH_DEV, LAGS), placed),
-            scratch_shapes=[pltpu.VMEM((2 * CH_DEV * PITCH, CH_DEV), jnp.float32)] * 2
-            + [pltpu.VMEM((SRC_STEP, LAGS, CH_DEV), jnp.bfloat16)],
-        ),
+        in_specs=[pl.BlockSpec(memory_space=pltpu.SMEM)] + [vmem] * 4,
+        out_specs=pl.BlockSpec(memory_space=pl.ANY),
         out_shape=jax.ShapeDtypeStruct((2, CH_DEV, CH_DEV, LAGS), jnp.bfloat16),
+        scratch_shapes=[pltpu.VMEM((2 * CH_DEV * PITCH, CH_DEV), jnp.float32)] * 2
+        + [
+            pltpu.VMEM((2 * CH_DEV, CH_DEV, LAGS), jnp.bfloat16),
+            pltpu.SemaphoreType.DMA((2 * CH_DEV // PIECE,)),
+        ],
         name="correlate",
-        compiler_params=pltpu.CompilerParams(vmem_limit_bytes=40 * 1024 * 1024),
+        compiler_params=pltpu.CompilerParams(vmem_limit_bytes=44 * 1024 * 1024),
     )(parity, here, there, own, inverse)
 
 

time: 49.6 us -> 45.9 us (0.925)
  Pallas kernels: 27.4 us -> 23.7 us
    pallas_call x1, Pallas kernels: 12.5 us -> 8.76 us  [correlate(): pl.pallas_call(correlate_kernel, in_specs=[pl.BlockSpec(memory_space=pltp...]
  transfers between devices with their start and end apart: 2 -> 2, of which waited for: 1 -> 1; matrix products, arithmetic and copies ran while one was open for 9% -> 10% of each run, Pallas kernels for 12% -> 13%
where the time goes in v3:
time: 45.9 us; the launch traced here: 45.6 us
  Pallas kernels  23.7 us (52%)
  waiting for transfers between devices  9.52 us (21%)
  starting transfers between devices  7.63 us (17%)
  other arithmetic  3.07 us (7%)
  local copies, waits for them, and re-layouts  1.6 us (3%)
    pallas_call x2, Pallas kernels, whiten(): pl.pallas_call(functools.partial(whiten_kernel, column, rounded), out_sha...  13.1 us
    all_to_all x1, waiting for transfers between devices, local(): lax.all_to_all(sent, 'ch', split_axis=0, concat_axis=0, tiled=True)  9.51 us
    pallas_call x1, Pallas kernels, correlate(): pl.pallas_call(correlate_kernel, in_specs=[pl.BlockSpec(memory_space=pltp...  8.76 us
    all_to_all x1, starting transfers between devices, local(): lax.all_to_all(sent, 'ch', split_axis=0, concat_axis=0, tiled=True)  7.41 us
    pallas_call x1, Pallas kernels, pack(): pl.pallas_call(pack_kernel, out_shape=jax.ShapeDtypeStruct((blocks, rows,...  1.85 us
    another operation x2, other arithmetic  1.59 us
    dynamic_slice x1, local copies, waits for them, and re-layouts, local(): own_source = lax.dynamic_slice_in_dim(source_order, parity, 1, 0)  1.31 us
  transfers between devices with their start and end apart: 2, of which 1 were waited for; matrix products, arithmetic and copies ran while one was open for 10% of the time, Pallas kernels for 13%

profile of v3, /device:TPU:0, one launch (start us, length us, event | category | flops | bytes accessed | tf_op | source)
XLA Modules:
  0.0 45.6 jit_solution(15176202504357948064)
XLA Ops:
  0.0 1.9 %pack.1 = bf16[16,64,256]{2,1,0:T(8,128)(2,1)} custom-call(s32[2]{0:T(128)} %order_ref.1, bf16[64,2048]{1,0:T(8,128)(2,1)} %x_ref.1), custom_call_target="tpu_custom_call" | custom-call | tf_op jit(solution)/shard_map/pack/pallas_call | solution.py:70
  1.9 7.4 %all-to-all-start = ((bf16[16,64,256]{2,1,0:T(8,128)(2,1)}), bf16[16,64,256]{2,1,0:T(8,128)(2,1)S(1)}, u32[]{:S(2)}, u32[]{:S(2)}) async-start(bf16[16,64,256]{2,1,0:T(8,128)(2,1)} %pack.1), calls=%async_computation | async-start | bytes 1048576 | tf_op jit(solution)/shard_map/all_to_all | solution.py:281
  9.4 1.3 %dynamic_slice.3.block_ref = s32[1]{0:T(128)} dynamic-slice(s32[2]{0:T(128)} %order_ref.1, s32[]{:T(128)S(6)} %select_n.29), dynamic_slice_sizes={1} | dynamic-slice | bytes 12 | tf_op jit(solution)/shard_map/dynamic_slice | solution.py:295
  10.7 0.7 %convert_element_type.33 = f32[2048]{0:T(1024)S(1)} convert(s32[2048]{0:T(1024)} %param.5) | non-fusion elementwise | flops 2048 | bytes 16384 | tf_op jit(solution)/shard_map/convert_element_type | solution.py:286
  11.4 0.3 cosine_convert_fusion.1
  11.8 1.2 %cosine_convert_fusion = (bf16[128,512]{1,0:T(8,128)(2,1)S(1)}, bf16[128,512]{1,0:T(8,128)(2,1)S(1)}) fusion(s32[128]{0:T(128)S(1)} %get-tuple-element.25), kind=kLoop, calls=%fused_computation.8 | loop fusion | flops 1114112 | bytes 262656 | tf_op jit(solution)/shard_map/convert.1
  13.1 0.7 %broadcast_clamp_fusion.starts_ref = s32[32]{0:T(128)S(1)} fusion(s32[32]{0:T(128)} %param.6), kind=kLoop, calls=%fused_computation.40 | loop fusion | flops 32 | bytes 256 | tf_op jit(solution)/shard_map/jit(clip)/min | solution.py:285
  13.7 0.1 broadcast_in_dim.13.fcount_ref
  13.8 0.1 broadcast_in_dim.12.tcount_ref
  13.9 0.1 copy.5.first_ref
  14.0 9.5 %all-to-all-done = bf16[16,64,256]{2,1,0:T(8,128)(2,1)S(1)} async-done(((bf16[16,64,256]{2,1,0:T(8,128)(2,1)}), bf16[16,64,256]{2,1,0:T(8,128)(2,1)S(1)}, u32[]{:S(2)}, u32[]{:S(2)}) %all-to-all-start) | async-done | bytes 524320 | tf_op jit(solution)/shard_map/all_to_all | solution.py:281
  23.5 7.0 %whiten.2.here_ref = bf16[128,64,128]{2,1,0:T(8,128)(2,1)S(1)} custom-call(s32[32]{0:T(128)S(1)} %broadcast_clamp_fusion.starts_ref, s32[1]{0:T(128)} %dynamic_slice.3.block_ref, bf16[1024,256]{1,0:T(8,128)(2,1)S(1)} %bitcast.5, s32[32,1]{1,0:T(8,128)S(1)} %copy.5.first_ref, f32[1,2048]{1,0:T(1,128)S(1)} %bitcast.7, ...), custom_call_target="tpu_custom_call" | custom-call | flops 6000000000 | bytes 3000000 | tf_op jit(solution)/shard_map/whiten/pallas_call | solution.py:182
  30.5 0.2 collective-permute-start
  30.8 6.1 %whiten.3.own_ref = f32[8320,128]{1,0:T(8,128)S(1)} custom-call(s32[32]{0:T(128)S(1)} %broadcast_clamp_fusion.starts_ref, s32[1]{0:T(128)} %bitcast.4.block_ref, bf16[1024,256]{1,0:T(8,128)(2,1)S(1)} %bitcast.6, s32[32,1]{1,0:T(8,128)S(1)} %copy.5.first_ref, f32[1,2048]{1,0:T(1,128)S(1)} %bitcast.8, bf16[256,512]{1,0:T(8,128)(2,1)S(1)} %pad_maximum_fusion.forward_ref, ...), custom_call_target="tpu_custom_call" | custom-call | flops 6000000000 | bytes 3000000 | tf_op jit(solution)/shard_map/whiten/pallas_call | solution.py:182
  36.8 0.0 collective-permute-done.there_ref
  36.8 8.8 %correlate.1 = bf16[2,128,128,128]{3,2,1,0:T(8,128)(2,1)} custom-call(s32[1]{0:T(128)} %bitcast.parity_ref, bf16[128,64,128]{2,1,0:T(8,128)(2,1)S(1)} %whiten.2.here_ref, bf16[128,64,128]{2,1,0:T(8,128)(2,1)S(1)} %collective-permute-done.there_ref, f32[8320,128]{1,0:T(8,128)S(1)} %whiten.3.own_ref, bf16[128,256]{1,0:T(8,128)(2,1)S(1)} %maximum_multiply_fusion.inverse_ref), custom_call_target="tpu_custom_call" | custom-call | tf_op jit(solution)/shard_map/correlate/pallas_call | solution.py:261
  (7 shorter events, 0.1 us)
Async XLA Ops:
  1.9 21.7 %all-to-all-start = ((bf16[16,64,256]{2,1,0:T(8,128)(2,1)}), bf16[16,64,256]{2,1,0:T(8,128)(2,1)S(1)}, u32[]{:S(2)}, u32[]{:S(2)}) async-start(bf16[16,64,256]{2,1,0:T(8,128)(2,1)} %pack.1), calls=%async_computation | async-start | bytes 1048576 | tf_op jit(solution)/shard_map/all_to_all | solution.py:281
  30.5 6.3 %collective-permute-start = (bf16[128,64,128]{2,1,0:T(8,128)(2,1)S(1)}, bf16[128,64,128]{2,1,0:T(8,128)(2,1)S(1)}, u32[]{:S(2)}, u32[]{:S(2)}) collective-permute-start(bf16[128,64,128]{2,1,0:T(8,128)(2,1)S(1)} %whiten.2.here_ref), channel_id=1, source_target_pairs={{0,1},{1,0},{2,3},{3,2},{4,5},{5,4},{6,7},{7,6},{8,9},{9,8},{10,11... | collective-permute-start | bytes 6291464 | tf_op jit(solution)/shard_map/ppermute | solution.py:298

commit v4 on v3

--- a/solution.py
+++ b/solution.py
@@ -19,9 +19,9 @@
 STABILIZER_FLOOR = 1e-06
 TILE = 128
 SPAN = TILE + 2 * HALF
-SRC_STEP = 128
+SRC_STEP = 256
 PIECE = 16
-BIN_STEP = 64
+BIN_STEP = 128
 PITCH = NF + 1
 
 

time: 45.9 us -> 45.8 us (level)
  no operation moved by 1% of the time
where the time goes in v4:
time: 45.8 us; the launch traced here: 45.6 us
  Pallas kernels  23.5 us (51%)
  waiting for transfers between devices  9.52 us (21%)
  starting transfers between devices  7.62 us (17%)
  other arithmetic  3.07 us (7%)
  local copies, waits for them, and re-layouts  1.6 us (3%)
    pallas_call x2, Pallas kernels, whiten(): pl.pallas_call(functools.partial(whiten_kernel, column, rounded), out_sha...  13.2 us
    all_to_all x1, waiting for transfers between devices, local(): lax.all_to_all(sent, 'ch', split_axis=0, concat_axis=0, tiled=True)  9.51 us
    pallas_call x1, Pallas kernels, correlate(): pl.pallas_call(correlate_kernel, in_specs=[pl.BlockSpec(memory_space=pltp...  8.39 us
    all_to_all x1, starting transfers between devices, local(): lax.all_to_all(sent, 'ch', split_axis=0, concat_axis=0, tiled=True)  7.41 us
    pallas_call x1, Pallas kernels, pack(): pl.pallas_call(pack_kernel, out_shape=jax.ShapeDtypeStruct((blocks, rows,...  1.85 us
    another operation x2, other arithmetic  1.59 us
    dynamic_slice x1, local copies, waits for them, and re-layouts, local(): own_source = lax.dynamic_slice_in_dim(source_order, parity, 1, 0)  1.31 us
  transfers between devices with their start and end apart: 2, of which 1 were waited for; matrix products, arithmetic and copies ran while one was open for 10% of the time, Pallas kernels for 13%

profile of v4, /device:TPU:0, one launch (start us, length us, event | category | flops | bytes accessed | tf_op | source)
XLA Modules:
  0.0 45.6 jit_solution(4294020487984554637)
XLA Ops:
  0.0 1.8 %pack.1 = bf16[16,64,256]{2,1,0:T(8,128)(2,1)} custom-call(s32[2]{0:T(128)} %order_ref.1, bf16[64,2048]{1,0:T(8,128)(2,1)} %x_ref.1), custom_call_target="tpu_custom_call" | custom-call | tf_op jit(solution)/shard_map/pack/pallas_call | solution.py:70
  1.8 7.4 %all-to-all-start = ((bf16[16,64,256]{2,1,0:T(8,128)(2,1)}), bf16[16,64,256]{2,1,0:T(8,128)(2,1)S(1)}, u32[]{:S(2)}, u32[]{:S(2)}) async-start(bf16[16,64,256]{2,1,0:T(8,128)(2,1)} %pack.1), calls=%async_computation | async-start | bytes 1048576 | tf_op jit(solution)/shard_map/all_to_all | solution.py:281
  9.4 1.3 %dynamic_slice.3.block_ref = s32[1]{0:T(128)} dynamic-slice(s32[2]{0:T(128)} %order_ref.1, s32[]{:T(128)S(6)} %select_n.29), dynamic_slice_sizes={1} | dynamic-slice | bytes 12 | tf_op jit(solution)/shard_map/dynamic_slice | solution.py:295
  10.7 0.7 %convert_element_type.33 = f32[2048]{0:T(1024)S(1)} convert(s32[2048]{0:T(1024)} %param.5) | non-fusion elementwise | flops 2048 | bytes 16384 | tf_op jit(solution)/shard_map/convert_element_type | solution.py:286
  11.4 0.3 cosine_convert_fusion.1
  11.8 1.2 %cosine_convert_fusion = (bf16[128,512]{1,0:T(8,128)(2,1)S(1)}, bf16[128,512]{1,0:T(8,128)(2,1)S(1)}) fusion(s32[128]{0:T(128)S(1)} %get-tuple-element.25), kind=kLoop, calls=%fused_computation.8 | loop fusion | flops 1114112 | bytes 262656 | tf_op jit(solution)/shard_map/convert.1
  13.1 0.7 %broadcast_clamp_fusion.starts_ref = s32[32]{0:T(128)S(1)} fusion(s32[32]{0:T(128)} %param.6), kind=kLoop, calls=%fused_computation.40 | loop fusion | flops 32 | bytes 256 | tf_op jit(solution)/shard_map/jit(clip)/min | solution.py:285
  13.7 0.1 broadcast_in_dim.13.fcount_ref
  13.8 0.1 broadcast_in_dim.12.tcount_ref
  13.9 0.1 copy.5.first_ref
  14.0 9.5 %all-to-all-done = bf16[16,64,256]{2,1,0:T(8,128)(2,1)S(1)} async-done(((bf16[16,64,256]{2,1,0:T(8,128)(2,1)}), bf16[16,64,256]{2,1,0:T(8,128)(2,1)S(1)}, u32[]{:S(2)}, u32[]{:S(2)}) %all-to-all-start) | async-done | bytes 524320 | tf_op jit(solution)/shard_map/all_to_all | solution.py:281
  23.5 7.2 %whiten.2.here_ref = bf16[128,64,128]{2,1,0:T(8,128)(2,1)S(1)} custom-call(s32[32]{0:T(128)S(1)} %broadcast_clamp_fusion.starts_ref, s32[1]{0:T(128)} %dynamic_slice.3.block_ref, bf16[1024,256]{1,0:T(8,128)(2,1)S(1)} %bitcast.5, s32[32,1]{1,0:T(8,128)S(1)} %copy.5.first_ref, f32[1,2048]{1,0:T(1,128)S(1)} %bitcast.7, ...), custom_call_target="tpu_custom_call" | custom-call | flops 6000000000 | bytes 3000000 | tf_op jit(solution)/shard_map/whiten/pallas_call | solution.py:182
  30.7 0.2 collective-permute-start
  30.9 6.1 %whiten.3.own_ref = f32[8320,128]{1,0:T(8,128)S(1)} custom-call(s32[32]{0:T(128)S(1)} %broadcast_clamp_fusion.starts_ref, s32[1]{0:T(128)} %bitcast.4.block_ref, bf16[1024,256]{1,0:T(8,128)(2,1)S(1)} %bitcast.6, s32[32,1]{1,0:T(8,128)S(1)} %copy.5.first_ref, f32[1,2048]{1,0:T(1,128)S(1)} %bitcast.8, bf16[256,512]{1,0:T(8,128)(2,1)S(1)} %pad_maximum_fusion.forward_ref, ...), custom_call_target="tpu_custom_call" | custom-call | flops 6000000000 | bytes 3000000 | tf_op jit(solution)/shard_map/whiten/pallas_call | solution.py:182
  37.0 0.0 collective-permute-done.there_ref
  37.0 8.4 %correlate.1 = bf16[2,128,128,128]{3,2,1,0:T(8,128)(2,1)} custom-call(s32[1]{0:T(128)} %bitcast.parity_ref, bf16[128,64,128]{2,1,0:T(8,128)(2,1)S(1)} %whiten.2.here_ref, bf16[128,64,128]{2,1,0:T(8,128)(2,1)S(1)} %collective-permute-done.there_ref, f32[8320,128]{1,0:T(8,128)S(1)} %whiten.3.own_ref, bf16[128,256]{1,0:T(8,128)(2,1)S(1)} %maximum_multiply_fusion.inverse_ref), custom_call_target="tpu_custom_call" | custom-call | tf_op jit(solution)/shard_map/correlate/pallas_call | solution.py:261
  (7 shorter events, 0.1 us)
Async XLA Ops:
  1.8 21.7 %all-to-all-start = ((bf16[16,64,256]{2,1,0:T(8,128)(2,1)}), bf16[16,64,256]{2,1,0:T(8,128)(2,1)S(1)}, u32[]{:S(2)}, u32[]{:S(2)}) async-start(bf16[16,64,256]{2,1,0:T(8,128)(2,1)} %pack.1), calls=%async_computation | async-start | bytes 1048576 | tf_op jit(solution)/shard_map/all_to_all | solution.py:281
  30.7 6.3 %collective-permute-start = (bf16[128,64,128]{2,1,0:T(8,128)(2,1)S(1)}, bf16[128,64,128]{2,1,0:T(8,128)(2,1)S(1)}, u32[]{:S(2)}, u32[]{:S(2)}) collective-permute-start(bf16[128,64,128]{2,1,0:T(8,128)(2,1)S(1)} %whiten.2.here_ref), channel_id=1, source_target_pairs={{0,1},{1,0},{2,3},{3,2},{4,5},{5,4},{6,7},{7,6},{8,9},{9,8},{10,11... | collective-permute-start | bytes 6291464 | tf_op jit(solution)/shard_map/ppermute | solution.py:298
